TPU v7x, 256 devices: a whole 4x4x8 slice. The times are simulated.
256 devices in a mesh: freq: 128 (over x, y, z_hi, core), plane: 2 (over z_lo).
Axes of the slice: x: 4, y: 4, z: 8 (z_hi: 4, z_lo: 2; z = z_hi * 2 + z_lo), core: 2. Of those that a mesh axis runs over, the one named last changes fastest.
Arguments:
- state_in: float32 [2, 256, 5, 256, 128], P(None, 'freq', None, 'plane'), may hold values from -6 to 6
- forcing_in: float32 [2, 256, 5, 256, 128], P(None, 'freq', None, 'plane'), may hold values from -6 to 6
- base_flow: float32 [128, 5, 256, 128], P('freq', None, 'plane'), may hold values from -1 to 1
- station_index: int32 [2], replicated, may hold values from 0 to 127
- lobe_count: int32 [1], replicated, may hold values from 3 to 127
Outputs:
- state_out: float32 [2, 256, 5, 256, 128], P(None, 'freq', None, 'plane')
- forcing_out: float32 [2, 256, 5, 256, 128], P(None, 'freq', None, 'plane')
All inputs are finite; a program needn't handle non-finite values.
Results may differ from a plain program's by a relative error of at most 0.0003.
Values sent between devices are 32-bit elements; how exact they have to be, the bound alone decides.
No kernel may reach another device: no remote copies, remote signals or barrier semaphores. Data moves between devices by JAX's collectives and lax.ppermute only.
A program may use at most 128 MiB of HBM per device.

v0:
```python
import math
import jax
import jax.numpy as jnp
from jax import lax
from jax.sharding import PartitionSpec as P

SWEEPS = 4
STEPS = 2
SIDE_WEIGHT = 1.25
MARCH_WEIGHT = 4.0
DIAG_SHIFT = 4.0
ADVECT_SCALE = 0.5
BASE_SCALE = 0.5
HIGHEST_MODE = lax.Precision.HIGHEST


def broadcast(value, axis, source):
    kept = jnp.where(lax.axis_index(axis) == source, value, 0).astype(value.dtype)
    return lax.psum(kept, axis)


def padded_2(cells, sides, width):
    for axis, dim in sides:
        count = lax.axis_size(axis)
        head = lax.slice_in_dim(cells, 0, width, axis=dim)
        tail = lax.slice_in_dim(cells, cells.shape[dim] - width, cells.shape[dim], axis=dim)
        cells = jnp.concatenate(
            [
                lax.ppermute(tail, axis, [(i, (i + 1) % count) for i in range(count)]),
                cells,
                lax.ppermute(head, axis, [((i + 1) % count, i) for i in range(count)]),
            ],
            axis=dim,
        )
    return cells


def radial_tables(radius_count):
    indices = jnp.arange(radius_count)
    angles = math.pi * indices.astype(jnp.float32) / (radius_count - 1)
    cheb_nodes = jnp.cos(angles)
    weights = jnp.where((indices == 0) | (indices == radius_count - 1), 2.0, 1.0).astype(
        jnp.float32
    )
    parity = (1 - 2 * ((indices[:, None] + indices[None, :]) % 2)).astype(jnp.float32)
    offdiag = indices[:, None] != indices[None, :]
    spacing = jnp.where(offdiag, cheb_nodes[:, None] - cheb_nodes[None, :], 1.0)
    entries = jnp.where(offdiag, weights[:, None] / weights[None, :] * parity / spacing, 0.0)
    entries = entries - jnp.diag(jnp.sum(entries, axis=1))
    slopes = jnp.sin(angles)[:, None] * entries / (radius_count - 1)
    stiffness = jnp.dot(slopes.T, slopes, precision=HIGHEST_MODE)
    system = stiffness + DIAG_SHIFT * jnp.eye(radius_count, dtype=jnp.float32)
    factor = jnp.linalg.cholesky(system)
    factor_inv = lax.linalg.triangular_solve(
        factor, jnp.eye(radius_count, dtype=jnp.float32), left_side=True, lower=True
    )
    return (slopes, jnp.dot(factor_inv.T, factor_inv, precision=HIGHEST_MODE))


def transform_tables(freqs, ntime):
    mode_ids = jnp.arange(freqs)
    time_ids = jnp.arange(ntime)
    phases = mode_ids[:, None] * time_ids[None, :] % ntime
    angles = 2.0 * math.pi * phases.astype(jnp.float32) / ntime
    cosines = jnp.cos(angles)
    sine_tab = jnp.sin(angles)
    stacked = jnp.concatenate([cosines, -sine_tab], axis=0)
    return (stacked.T / math.sqrt(freqs), stacked / math.sqrt(ntime))


def chevron(lobe_count, azimuths, start_az, total_az):
    position = start_az + jnp.arange(azimuths)
    phases = lobe_count[0] * position % total_az
    return 1.0 + 0.5 * jnp.cos(2.0 * math.pi * phases.astype(jnp.float32) / total_az)


def relax_sweep(inner, neighbours, right_side, coefficient, omegas, inverse_p):
    real_part = inner[0]
    imag_part = inner[1]
    rate_col = omegas[:, None, None, None]
    scaled = coefficient[None]
    mixing = jnp.stack(
        [scaled * real_part - rate_col * imag_part, scaled * imag_part + rate_col * real_part]
    )
    summed = right_side - mixing + SIDE_WEIGHT * neighbours
    radius_count = summed.shape[-1]
    return jnp.dot(summed.reshape(-1, radius_count), inverse_p.T, precision=HIGHEST_MODE).reshape(
        summed.shape
    )


def advect(velocity, radial_time, around_time):
    carried = velocity[:, 1:2] * radial_time + velocity[:, 2:3] * around_time
    spread = velocity[:, 0] * (radial_time[:, 1] + around_time[:, 2])
    carried = jnp.concatenate([carried[:, 0:1] + spread[:, None], carried[:, 1:]], axis=1)
    return -ADVECT_SCALE * carried


def per_device(state_in, forcing_in, base_flow, station_index, lobe_count):
    per_dev = state_in.shape[1]
    variables = state_in.shape[2]
    span_az = state_in.shape[3]
    radius_count = state_in.shape[4]
    freqs = per_dev * lax.axis_size("freq")
    ntime = 3 * freqs // 2
    slopes, inverse_p = radial_tables(radius_count)
    inverse, forward = transform_tables(freqs, ntime)
    first_mode = lax.axis_index("freq") * per_dev
    omegas = 0.5 * (first_mode + jnp.arange(per_dev)).astype(jnp.float32) / freqs
    shape_az = chevron(
        lobe_count, span_az, lax.axis_index("plane") * span_az, span_az * lax.axis_size("plane")
    )
    stored = base_flow.shape[0]
    march_state = state_in
    forcing = forcing_in
    for station in range(STEPS):
        wanted = station_index[station]
        local_plane = lax.dynamic_index_in_dim(base_flow, wanted % stored, 0, keepdims=False)
        plane_flow = broadcast(local_plane, "freq", wanted // stored)
        coefficient = BASE_SCALE * plane_flow * shape_az[None, :, None]
        right_side = MARCH_WEIGHT * march_state + forcing
        iterate = march_state
        for sweep_no in range(SWEEPS):
            padded = padded_2(iterate, (("plane", 3),), 1)
            iterate = relax_sweep(
                iterate,
                padded[:, :, :, 2:] + padded[:, :, :, :-2],
                right_side,
                coefficient,
                omegas,
                inverse_p,
            )
        march_state = iterate
        rimmed = padded_2(march_state, (("plane", 3),), 1)
        beside_all = 0.5 * (rimmed[:, :, :, 2:] - rimmed[:, :, :, :-2])
        radial = jnp.dot(
            march_state.reshape(-1, radius_count), slopes.T, precision=HIGHEST_MODE
        ).reshape(march_state.shape)
        fields = jnp.stack([march_state, radial, beside_all])
        points = lax.all_to_all(fields, "freq", split_axis=4, concat_axis=2, tiled=True)
        in_time = jnp.einsum(
            "tc,kcx->ktx", inverse, points.reshape(3, 2 * freqs, -1), precision=HIGHEST_MODE
        ).reshape(3, ntime, variables, -1)
        velocity = in_time[0]
        radial_time = in_time[1]
        around_time = in_time[2]
        source = advect(velocity, radial_time, around_time)
        spectral = jnp.dot(forward, source.reshape(ntime, -1), precision=HIGHEST_MODE).reshape(
            2, freqs, variables, -1, radius_count
        )
        forcing = lax.all_to_all(spectral, "freq", split_axis=1, concat_axis=3, tiled=True)
    return (march_state, forcing)


def solution(mesh):
    return jax.shard_map(
        per_device,
        mesh=mesh,
        in_specs=(
            P(None, "freq", None, "plane", None),
            P(None, "freq", None, "plane", None),
            P("freq", None, "plane", None),
            P(),
            P(),
        ),
        out_specs=(P(None, "freq", None, "plane", None), P(None, "freq", None, "plane", None)),
        check_vma=False,
    )
```

profile of v0, /device:TPU:32, one launch (start us, length us, event | category | flops | bytes accessed | tf_op | source)
XLA Modules:
  0.0 1701.8 jit_solution(14322298090802658548)
XLA Ops:
  8.2 1.9 collective-permute-start
  10.3 1.3 fusion.125
  12.9 1.9 select_bitcast_fusion
  16.3 11.7 cholesky.18
  29.4 9.8 custom-call.6
  39.8 1249.7 %all-reduce.3.cloned.1.call-done = (f32[5,128,128]{2,1,0:T(8,128)}, f32[5,128,128]{2,1,0:T(8,128)}) async-done(((f32[5,128,128]{2,1,0:T(8,128)}, f32[5,128,128]{2,1,0:T(8,128)}), (f32[5,128,128]{2,1,0:T(8,128)}, f32[5,128,128]{2,1,0:T(8,128)})) %all-reduce.3.cloned.1.call-update) | async-done | bytes 655376 | tf_op jit(solution)/shard_map/psum | solution.py:19
  1289.5 1.2 broadcast_multiply_fusion
  1293.8 1.5 collective-permute-start.2
  1297.6 1.8 collective-permute-done.3
  1299.9 1.2 fusion.128
  1302.0 1.4 collective-permute-start.5
  1303.7 1.3 collective-permute-done.4
  1307.5 1.5 collective-permute-start.6
  1310.0 1.3 collective-permute-done.6
  1311.3 1.4 collective-permute-done.7
  1315.2 1.5 collective-permute-start.9
  1316.7 1.3 fusion.67
  1319.7 4.9 copy.116
  1324.6 7.3 all-to-all-start
  1331.9 1.6 sine_negate_fusion
  1333.6 75.5 %all-to-all-done = f32[3,2,2,5,128,128]{5,2,3,1,0,4:T(2,128)} async-done(((f32[3,2,2,5,128,128]{5,2,3,1,0,4:T(2,128)}), f32[3,2,2,5,128,128]{5,2,3,1,0,4:T(2,128)}, u32[]{:S(2)}, u32[]{:S(2)}) %all-to-all-start) | async-done | bytes 3932192 | tf_op jit(solution)/shard_map/all_to_all | solution.py:140
  1409.2 5.6 copy.117
  1414.8 6.8 reshape.545
  1421.6 8.6 convolution_bitcast_fusion.1
  1430.8 2.5 convolution_bitcast_fusion.3
  1433.3 2.1 copy.119
  1435.4 21.5 %all-to-all-start.1 = ((f32[2,256,5,1,128]{4,0,3,2,1:T(2,128)}), f32[2,256,5,1,128]{4,0,3,2,1:T(2,128)S(1)}, u32[]{:S(2)}, u32[]{:S(2)}) async-start(f32[2,256,5,1,128]{4,0,3,2,1:T(2,128)} %copy.119), calls=%async_computation.1 | async-start | bytes 2621440 | tf_op jit(solution)/shard_map/all_to_all | solution.py:151
  1457.0 1.3 multiply_subtract_fusion.3
  1458.3 30.5 %all-to-all-done.1 = f32[2,256,5,1,128]{4,0,3,2,1:T(2,128)S(1)} async-done(((f32[2,256,5,1,128]{4,0,3,2,1:T(2,128)}), f32[2,256,5,1,128]{4,0,3,2,1:T(2,128)S(1)}, u32[]{:S(2)}, u32[]{:S(2)}) %all-to-all-start.1) | async-done | bytes 1310752 | tf_op jit(solution)/shard_map/all_to_all | solution.py:151
  1488.9 1.7 fusion.24
  1491.9 7.1 collective-permute-start.10
  1499.5 1.2 collective-permute-done.10
  1500.7 2.0 collective-permute-done.11
  1504.7 1.9 collective-permute-start.13
  1507.0 1.3 collective-permute-done.12
  1510.2 2.0 collective-permute-start.14
  1514.0 2.1 collective-permute-done.15
  1516.6 1.2 fusion.134
  1518.0 1.9 collective-permute-start.17
  1519.9 1.3 fusion.66
  1522.2 3.0 copy.122
  1525.3 99.7 %all_to_all.66 = f32[3,2,2,5,128,128]{5,2,3,1,0,4:T(2,128)S(1)} all-to-all(f32[3,2,2,5,128,128]{5,2,3,1,0,4:T(2,128)S(1)} %copy.122), channel_id=1, replica_groups=mesh['freq'=128,'plane'=2] {'freq'}, dimensions={4} | all-to-all | bytes 7864320 | tf_op jit(solution)/shard_map/all_to_all | solution.py:140
  1624.9 3.5 copy.123
  1628.4 6.9 reshape.555
  1635.3 8.6 convolution_bitcast_fusion
  1645.5 2.5 convolution_bitcast_fusion.2
  1649.1 44.3 %all_to_all.67 = f32[2,256,5,1,128]{4,0,3,2,1:T(2,128)S(1)} all-to-all(f32[2,256,5,1,128]{4,0,3,2,1:T(2,128)S(1)} %copy.125), channel_id=1, replica_groups=mesh['freq'=128,'plane'=2] {'freq'}, dimensions={1} | all-to-all | bytes 2621440 | tf_op jit(solution)/shard_map/all_to_all | solution.py:151
  1693.3 1.2 copy.142
  (100 shorter events, 31.0 us)
Async XLA Ops:
  7.2 1282.3 %all-reduce.3.cloned.1.call-start = ((), (), s32[]{:S(2)}) async-start(), calls=%async_computation.4 | async-start | bytes 1310720 | tf_op jit(solution)/shard_map/psum | solution.py:19
  8.2 1282.9 %collective-permute-start = (f32[2,2,5,1,128]{4,3,2,1,0:T(1,128)S(1)}, f32[2,2,5,1,128]{4,3,2,1,0:T(1,128)S(1)}, u32[]{:S(2)}, u32[]{:S(2)}) collective-permute-start(f32[2,2,5,1,128]{4,3,2,1,0:T(1,128)S(1)} %get-tuple-element.56), channel_id=1, source_target_pairs={{1,0},{0,1},{3,2},{2,3},{5,4},{4,5},{7,6},{6,7},{9,8},{8,9},{11,10... | collective-permute-start | bytes 30728 | tf_op jit(solution)/shard_map/ppermute | solution.py:31
  10.1 1281.0 %collective-permute-start.1 = (f32[2,2,5,1,128]{4,3,2,1,0:T(1,128)S(1)}, f32[2,2,5,1,128]{4,3,2,1,0:T(1,128)S(1)}, u32[]{:S(2)}, u32[]{:S(2)}) collective-permute-start(f32[2,2,5,1,128]{4,3,2,1,0:T(1,128)S(1)} %get-tuple-element.57), channel_id=1, source_target_pairs={{0,1},{1,0},{2,3},{3,2},{4,5},{5,4},{6,7},{7,6},{8,9},{9,8},{10,11... | collective-permute-start | bytes 30728 | tf_op jit(solution)/shard_map/ppermute | solution.py:29
  16.1 1274.5 %copy-start = (f32[2,2,5,128,128]{4,3,2,1,0:T(8,128)S(1)}, f32[2,2,5,128,128]{4,3,2,1,0:T(8,128)}, u32[]{:S(2)}) copy-start(f32[2,2,5,128,128]{4,3,2,1,0:T(8,128)} %param.5) | copy-start | bytes 3932164
  1290.7 1.3 copy-start.2
  1293.8 3.8 collective-permute-start.2
  1295.3 4.1 collective-permute-start.3
  1301.2 3.8 collective-permute-start.4
  1302.0 3.7 collective-permute-start.5
  1307.5 3.8 collective-permute-start.6
  1309.0 3.7 collective-permute-start.7
  1314.4 3.8 collective-permute-start.8
  1315.2 3.8 collective-permute-start.9
  1324.6 84.6 %all-to-all-start = ((f32[3,2,2,5,128,128]{5,2,3,1,0,4:T(2,128)}), f32[3,2,2,5,128,128]{5,2,3,1,0,4:T(2,128)}, u32[]{:S(2)}, u32[]{:S(2)}) async-start(f32[3,2,2,5,128,128]{5,2,3,1,0,4:T(2,128)} %copy.116), calls=%async_computation | async-start | bytes 7864320 | tf_op jit(solution)/shard_map/all_to_all | solution.py:140
  1333.5 88.1 %copy-start.5 = (f32[256,384]{1,0:T(8,128)}, f32[256,384]{1,0:T(8,128)S(1)}, u32[]{:S(2)}) copy-start(f32[256,384]{1,0:T(8,128)S(1)} %get-tuple-element.71) | copy-start | bytes 1179652
  1333.6 97.2 %copy-start.3 = (f32[512,384]{1,0:T(8,128)}, f32[512,384]{1,0:T(8,128)S(1)}, u32[]{:S(2)}) copy-start(f32[512,384]{1,0:T(8,128)S(1)} %fusion.37) | copy-start | bytes 2359300
  1435.4 53.5 %all-to-all-start.1 = ((f32[2,256,5,1,128]{4,0,3,2,1:T(2,128)}), f32[2,256,5,1,128]{4,0,3,2,1:T(2,128)S(1)}, u32[]{:S(2)}, u32[]{:S(2)}) async-start(f32[2,256,5,1,128]{4,0,3,2,1:T(2,128)} %copy.119), calls=%async_computation.1 | async-start | bytes 2621440 | tf_op jit(solution)/shard_map/all_to_all | solution.py:151
  1491.9 8.8 collective-permute-start.10
  1499.1 3.7 collective-permute-start.11
  1504.5 3.8 collective-permute-start.12
  1504.7 3.7 collective-permute-start.13
  1510.2 3.8 collective-permute-start.14
  1512.2 3.9 collective-permute-start.15
  1517.8 4.2 copy-start.1
  1517.8 3.8 collective-permute-start.16
  1518.0 3.7 collective-permute-start.17
  1628.4 6.9 copy-start.6
  1644.4 1.1 copy-start.4
Sparse Core Ops, SparseCore 0:
  14.9 1274.5 all-reduce.2
where the time goes:
time: 1710 us; the launch traced here: 1700 us
  waiting for transfers between devices  1370 us (80%)
  blocking collectives  144 us (8%)
  starting transfers between devices  53.8 us (3%)
  local copies, waits for them, and re-layouts  40.7 us (2%)
  other arithmetic  38.3 us (2%)
  matrix products  35.5 us (2%)
    psum x1, waiting for transfers between devices, broadcast(): return lax.psum(kept, axis)  1250 us
    all_to_all x1, blocking collectives, per_device(): lax.all_to_all(fields, 'freq', split_axis=4, concat_axis=2, tiled=True)  99.7 us
    all_to_all x1, waiting for transfers between devices, per_device(): lax.all_to_all(fields, 'freq', split_axis=4, concat_axis=2, tiled=True)  75.5 us
    all_to_all x1, blocking collectives, per_device(): lax.all_to_all(spectral, 'freq', split_axis=1, concat_axis=3, tiled=True)  44.3 us
  transfers between devices with their start and end apart: 21, of which 19 were waited for; matrix products, arithmetic and copies ran while one was open for 2% of the time, Pallas kernels for 0%

commit v1 on v0

--- a/solution.py
+++ b/solution.py
@@ -14,9 +14,13 @@
 HIGHEST_MODE = lax.Precision.HIGHEST
 
 
+def raise_heads_here(frame_in, chip_axis):
+    return lax.all_gather(frame_in, chip_axis).sum(axis=0)
+
+
 def broadcast(value, axis, source):
     kept = jnp.where(lax.axis_index(axis) == source, value, 0).astype(value.dtype)
-    return lax.psum(kept, axis)
+    return raise_heads_here(kept, axis)
 
 
 def padded_2(cells, sides, width):

time: 1710 us -> 859 us (0.50)
  waiting for transfers between devices: 1370 us -> 485 us
  other arithmetic: 38.3 us -> 66.6 us
    psum x1 -> x0, waiting for transfers between devices: 1250 us -> none  [broadcast(): return lax.psum(kept, axis)]
    all_gather x0 -> x2, waiting for transfers between devices: none -> 364 us  [raise_heads_here(): return lax.all_gather(frame_in, chip_axis).sum(axis=0)]
    reduce_sum x0 -> x2, other arithmetic: none -> 29.4 us  [raise_heads_here(): return lax.all_gather(frame_in, chip_axis).sum(axis=0)]
  transfers between devices with their start and end apart: 21 -> 22, of which waited for: 19 -> 20; matrix products, arithmetic and copies ran while one was open for 2% -> 7% of each run, Pallas kernels for 0% -> 0%
where the time goes in v1:
time: 859 us; the launch traced here: 850 us
  waiting for transfers between devices  485 us (56%)
  blocking collectives  144 us (17%)
  other arithmetic  66.6 us (8%)
  starting transfers between devices  61.8 us (7%)
  local copies, waits for them, and re-layouts  39.8 us (5%)
  matrix products  35.4 us (4%)
  between operations  17 us (2%)
    all_gather x2, waiting for transfers between devices, raise_heads_here(): return lax.all_gather(frame_in, chip_axis).sum(axis=0)  364 us
    all_to_all x1, blocking collectives, per_device(): lax.all_to_all(fields, 'freq', split_axis=4, concat_axis=2, tiled=True)  100 us
    all_to_all x1, waiting for transfers between devices, per_device(): lax.all_to_all(fields, 'freq', split_axis=4, concat_axis=2, tiled=True)  72.2 us
    all_to_all x1, blocking collectives, per_device(): lax.all_to_all(spectral, 'freq', split_axis=1, concat_axis=3, tiled=True)  44.3 us
    all_to_all x1, waiting for transfers between devices, per_device(): lax.all_to_all(spectral, 'freq', split_axis=1, concat_axis=3, tiled=True)  30.4 us
    reduce_sum x2, other arithmetic, raise_heads_here(): return lax.all_gather(frame_in, chip_axis).sum(axis=0)  29.4 us
    all_to_all x1, starting transfers between devices, per_device(): lax.all_to_all(spectral, 'freq', split_axis=1, concat_axis=3, tiled=True)  24.9 us
    dot_general x2, matrix products, per_device(): jnp.einsum('tc,kcx->ktx', inverse, points.reshape(3, 2 * freqs, -1), prec...  17.3 us
  transfers between devices with their start and end apart: 22, of which 20 were waited for; matrix products, arithmetic and copies ran while one was open for 7% of the time, Pallas kernels for 0%

profile of v1, /device:TPU:32, one launch (start us, length us, event | category | flops | bytes accessed | tf_op | source)
XLA Modules:
  0.0 849.7 jit_solution(8460665189627302789)
XLA Ops:
  7.2 1.3 fusion.125
  9.9 1.9 broadcast_select_fusion
  12.5 1.9 collective-permute-start.1
  16.2 11.7 %cholesky.18 = f32[128,128]{1,0:T(8,128)S(1)} custom-call(f32[128,128]{1,0:T(8,128)S(1)} %fusion.64), custom_call_target="Cholesky" | custom-call | tf_op jit(solution)/shard_map/jit(cholesky)/cholesky | solution.py:57
  29.1 9.8 %custom-call.6 = f32[1,128,128]{1,2,0:T(8,128)S(1)} custom-call(f32[1,128,128]{2,1,0:T(8,128)S(1)} %fusion.56), custom_call_target="InvertDiagBlocksLowerTriangular" | custom-call | tf_op jit(solution)/shard_map/triangular_solve | solution.py:58
  39.5 175.4 %all-gather.5.cloned.1.call-done = f32[128,5,128,128]{3,2,1,0:T(8,128)} async-done(((f32[1,5,128,128]{3,2,1,0:T(8,128)}), f32[128,5,128,128]{3,2,1,0:T(8,128)}) %all-gather.5.cloned.1.call-update) | async-done | bytes 41943056 | tf_op jit(solution)/shard_map/all_gather | solution.py:18
  215.0 14.7 %reduce_sum.29 = f32[5,128,128]{2,1,0:T(8,128)S(1)} reduce(f32[128,5,128,128]{3,2,1,0:T(8,128)} %all-gather.5.cloned.1.call-done, f32[]{:T(128)} %constant.158.clone.1), dimensions={0}, to_apply=%region_4.5 | reduce | flops 10403840 | bytes 42270724 | tf_op jit(solution)/shard_map/reduce_sum | solution.py:18
  229.7 189.0 %all-gather.3.cloned.1.call-done = f32[128,5,128,128]{3,2,1,0:T(8,128)} async-done(((f32[1,5,128,128]{3,2,1,0:T(8,128)}), f32[128,5,128,128]{3,2,1,0:T(8,128)}) %all-gather.3.cloned.1.call-update) | async-done | bytes 41943056 | tf_op jit(solution)/shard_map/all_gather | solution.py:18
  418.7 14.7 %reduce_sum.27 = f32[5,128,128]{2,1,0:T(8,128)S(1)} reduce(f32[128,5,128,128]{3,2,1,0:T(8,128)} %all-gather.3.cloned.1.call-done, f32[]{:T(128)} %constant.158.clone.1), dimensions={0}, to_apply=%region_0.1 | reduce | flops 10403840 | bytes 42270724 | tf_op jit(solution)/shard_map/reduce_sum | solution.py:18
  437.2 1.9 collective-permute-start.2
  443.2 1.6 collective-permute-start.5
  445.7 1.3 collective-permute-done.5
  447.0 1.5 collective-permute-done.4
  451.0 1.5 collective-permute-start.6
  452.8 1.3 collective-permute-done.7
  456.4 1.6 collective-permute-start.8
  458.7 1.3 fusion.67
  460.2 1.6 collective-permute-done.9
  462.5 4.9 copy.114
  467.4 11.7 %all-to-all-start = ((f32[3,2,2,5,128,128]{5,2,3,1,0,4:T(2,128)}), f32[3,2,2,5,128,128]{5,2,3,1,0,4:T(2,128)}, u32[]{:S(2)}, u32[]{:S(2)}) async-start(f32[3,2,2,5,128,128]{5,2,3,1,0,4:T(2,128)} %copy.114), calls=%async_computation | async-start | bytes 7864320 | tf_op jit(solution)/shard_map/all_to_all | solution.py:144
  479.1 1.6 sine_negate_fusion
  480.8 72.2 %all-to-all-done = f32[3,2,2,5,128,128]{5,2,3,1,0,4:T(2,128)} async-done(((f32[3,2,2,5,128,128]{5,2,3,1,0,4:T(2,128)}), f32[3,2,2,5,128,128]{5,2,3,1,0,4:T(2,128)}, u32[]{:S(2)}, u32[]{:S(2)}) %all-to-all-start) | async-done | bytes 3932192 | tf_op jit(solution)/shard_map/all_to_all | solution.py:144
  553.1 5.6 copy.115
  558.7 6.8 reshape.543
  565.5 8.6 %convolution_bitcast_fusion.1 = f32[3,384,640]{1,2,0:T(8,128)S(1)} fusion(f32[3,512,640]{2,1,0:T(8,128)} %reshape.543, f32[256,384]{1,0:T(8,128)S(1)} %get-tuple-element.68, f32[256,384]{1,0:T(8,128)S(1)} %get-tuple-element.69), kind=kOutput, calls=%fused_computation.3 | convolution fusion | flops 4530241536 | bytes 7667712 | tf_op jit(solution)/shard_map/tc,kcx->ktx/dot_general | solution.py:145
  574.7 2.5 convolution_bitcast_fusion.3
  577.2 2.1 copy.117
  579.3 24.9 %all-to-all-start.1 = ((f32[2,256,5,1,128]{4,0,3,2,1:T(2,128)}), f32[2,256,5,1,128]{4,0,3,2,1:T(2,128)S(1)}, u32[]{:S(2)}, u32[]{:S(2)}) async-start(f32[2,256,5,1,128]{4,0,3,2,1:T(2,128)} %copy.117), calls=%async_computation.1 | async-start | bytes 2621440 | tf_op jit(solution)/shard_map/all_to_all | solution.py:155
  604.3 1.3 multiply_subtract_fusion.3
  605.6 30.4 %all-to-all-done.1 = f32[2,256,5,1,128]{4,0,3,2,1:T(2,128)S(1)} async-done(((f32[2,256,5,1,128]{4,0,3,2,1:T(2,128)}), f32[2,256,5,1,128]{4,0,3,2,1:T(2,128)S(1)}, u32[]{:S(2)}, u32[]{:S(2)}) %all-to-all-start.1) | async-done | bytes 1310752 | tf_op jit(solution)/shard_map/all_to_all | solution.py:155
  636.0 1.7 fusion.24
  639.0 7.3 collective-permute-start.11
  646.8 1.2 collective-permute-done.11
  648.0 2.0 collective-permute-done.10
  652.0 1.9 collective-permute-start.12
  654.3 1.3 collective-permute-done.13
  657.5 2.0 collective-permute-start.15
  661.2 2.2 collective-permute-done.14
  665.2 2.0 collective-permute-start.16
  667.2 1.3 fusion.66
  669.7 3.0 copy.120
  672.7 100.2 %all_to_all.66 = f32[3,2,2,5,128,128]{5,2,3,1,0,4:T(2,128)S(1)} all-to-all(f32[3,2,2,5,128,128]{5,2,3,1,0,4:T(2,128)S(1)} %copy.120), channel_id=1, replica_groups=mesh['freq'=128,'plane'=2] {'freq'}, dimensions={4} | all-to-all | bytes 7864320 | tf_op jit(solution)/shard_map/all_to_all | solution.py:144
  772.9 3.5 copy.121
  776.4 6.9 reshape.553
  783.3 8.6 %convolution_bitcast_fusion = f32[3,384,640]{1,2,0:T(8,128)S(1)} fusion(f32[3,512,640]{2,1,0:T(8,128)} %reshape.553, f32[256,384]{1,0:T(8,128)S(1)} %get-tuple-element.68, f32[256,384]{1,0:T(8,128)S(1)} %copy-done.6), kind=kOutput, calls=%fused_computation.2 | convolution fusion | flops 4530241536 | bytes 7667712 | tf_op jit(solution)/shard_map/tc,kcx->ktx/dot_general | solution.py:145
  793.5 2.5 convolution_bitcast_fusion.2
  797.0 44.3 %all_to_all.67 = f32[2,256,5,1,128]{4,0,3,2,1:T(2,128)S(1)} all-to-all(f32[2,256,5,1,128]{4,0,3,2,1:T(2,128)S(1)} %copy.123), channel_id=1, replica_groups=mesh['freq'=128,'plane'=2] {'freq'}, dimensions={1} | all-to-all | bytes 2621440 | tf_op jit(solution)/shard_map/all_to_all | solution.py:155
  841.3 1.2 copy.140
  (105 shorter events, 32.5 us)
Async XLA Ops:
  7.2 5.4 copy-start
  7.2 207.8 %all-gather.5.cloned.1.call-start = ((), (), s32[]{:S(2)}) async-start(), calls=%async_computation.5 | async-start | bytes 42270720 | tf_op jit(solution)/shard_map/all_gather | solution.py:18
  11.8 406.9 %all-gather.3.cloned.1.call-start = ((), (), s32[]{:S(2)}) async-start(), calls=%async_computation.4 | async-start | bytes 42270720 | tf_op jit(solution)/shard_map/all_gather | solution.py:18
  12.5 421.3 %collective-permute-start.1 = (f32[2,2,5,1,128]{4,3,2,1,0:T(1,128)S(1)}, f32[2,2,5,1,128]{4,3,2,1,0:T(1,128)S(1)}, u32[]{:S(2)}, u32[]{:S(2)}) collective-permute-start(f32[2,2,5,1,128]{4,3,2,1,0:T(1,128)S(1)} %get-tuple-element.55), channel_id=1, source_target_pairs={{0,1},{1,0},{2,3},{3,2},{4,5},{5,4},{6,7},{7,6},{8,9},{9,8},{10,11... | collective-permute-start | bytes 30728 | tf_op jit(solution)/shard_map/ppermute | solution.py:33
  14.5 419.4 %collective-permute-start = (f32[2,2,5,1,128]{4,3,2,1,0:T(1,128)S(1)}, f32[2,2,5,1,128]{4,3,2,1,0:T(1,128)S(1)}, u32[]{:S(2)}, u32[]{:S(2)}) collective-permute-start(f32[2,2,5,1,128]{4,3,2,1,0:T(1,128)S(1)} %get-tuple-element.54), channel_id=1, source_target_pairs={{1,0},{0,1},{3,2},{2,3},{5,4},{4,5},{7,6},{6,7},{9,8},{8,9},{11,10... | collective-permute-start | bytes 30728 | tf_op jit(solution)/shard_map/ppermute | solution.py:35
  433.5 1.3 copy-start.2
  436.6 3.9 collective-permute-start.3
  437.2 4.1 collective-permute-start.2
  443.2 3.8 collective-permute-start.5
  444.8 3.7 collective-permute-start.4
  450.3 3.8 collective-permute-start.7
  451.0 3.7 collective-permute-start.6
  456.4 3.8 collective-permute-start.8
  458.0 3.8 collective-permute-start.9
  467.4 85.7 %all-to-all-start = ((f32[3,2,2,5,128,128]{5,2,3,1,0,4:T(2,128)}), f32[3,2,2,5,128,128]{5,2,3,1,0,4:T(2,128)}, u32[]{:S(2)}, u32[]{:S(2)}) async-start(f32[3,2,2,5,128,128]{5,2,3,1,0,4:T(2,128)} %copy.114), calls=%async_computation | async-start | bytes 7864320 | tf_op jit(solution)/shard_map/all_to_all | solution.py:144
  480.7 84.8 %copy-start.5 = (f32[256,384]{1,0:T(8,128)}, f32[256,384]{1,0:T(8,128)S(1)}, u32[]{:S(2)}) copy-start(f32[256,384]{1,0:T(8,128)S(1)} %get-tuple-element.69) | copy-start | bytes 1179652
  480.8 93.9 %copy-start.3 = (f32[512,384]{1,0:T(8,128)}, f32[512,384]{1,0:T(8,128)S(1)}, u32[]{:S(2)}) copy-start(f32[512,384]{1,0:T(8,128)S(1)} %fusion.37) | copy-start | bytes 2359300
  579.3 56.7 %all-to-all-start.1 = ((f32[2,256,5,1,128]{4,0,3,2,1:T(2,128)}), f32[2,256,5,1,128]{4,0,3,2,1:T(2,128)S(1)}, u32[]{:S(2)}, u32[]{:S(2)}) async-start(f32[2,256,5,1,128]{4,0,3,2,1:T(2,128)} %copy.117), calls=%async_computation.1 | async-start | bytes 2621440 | tf_op jit(solution)/shard_map/all_to_all | solution.py:155
  639.0 9.0 %collective-permute-start.11 = (f32[2,2,5,1,128]{4,3,2,1,0:T(1,128)S(1)}, f32[2,2,5,1,128]{4,3,2,1,0:T(1,128)S(1)}, u32[]{:S(2)}, u32[]{:S(2)}) collective-permute-start(f32[2,2,5,1,128]{4,3,2,1,0:T(1,128)S(1)} %get-tuple-element.37), channel_id=1, source_target_pairs={{0,1},{1,0},{2,3},{3,2},{4,5},{5,4},{6,7},{7,6},{8,9},{9,8},{10,11... | collective-permute-start | bytes 30728 | tf_op jit(solution)/shard_map/ppermute | solution.py:33
  646.3 3.7 collective-permute-start.10
  651.8 3.8 collective-permute-start.13
  652.0 3.7 collective-permute-start.12
  657.5 3.8 collective-permute-start.15
  659.5 3.9 collective-permute-start.14
  665.1 4.2 copy-start.1
  665.1 3.8 collective-permute-start.17
  665.2 3.8 collective-permute-start.16
  776.4 6.9 copy-start.6
  792.3 1.1 copy-start.4
Sparse Core Ops, SparseCore 0:
  12.2 202.7 all-gather.4
  219.1 199.5 all-gather.2
